TPU v7x, 512 devices: a whole 4x4x16 slice. The times are simulated.
512 devices in a mesh: batch: 64 (over z_lo, y, core), space: 8 (over x, z_hi).
Axes of the slice: x: 4, y: 4, z: 16 (z_hi: 2, z_lo: 8; z = z_hi * 8 + z_lo), core: 2. Of those that a mesh axis runs over, the one named last changes fastest.
Arguments:
- acts: bfloat16 [64, 32, 64, 640], P('batch', 'space'), may hold values from -6 to 6
- conv_weight: bfloat16 [5760, 640], P('batch', 'space'), may hold values from -0.078125 to 0.078125
- conv_bias: float32 [640], replicated, may hold values from -4 to 4
- out_cotangent: bfloat16 [64, 32, 64, 640], P('batch', 'space'), may hold values from -6 to 6
- basis_in: bfloat16 [5760, 64], P('batch'), may hold values from -0.078125 to 0.078125
- basis_out: bfloat16 [640, 64], P('batch'), may hold values from -0.25 to 0.25
- query_ids: int32 [8], replicated, may hold values from 0 to 63
Outputs:
- activated: bfloat16 [64, 32, 64, 640], P('batch', 'space')
- basis_in_new: bfloat16 [5760, 64], P('batch')
- scores: float32 [8, 64], P(None, 'batch')
All inputs are finite; a program needn't handle non-finite values.
Results may differ from a plain program's by a relative error of at most 0.0031.
Values may be sent and summed in bfloat16 or wider, within the bound.
No kernel may reach another device: no remote copies, remote signals or barrier semaphores. Data moves between devices by JAX's collectives and lax.ppermute only.
A program may use at most 64 MiB of HBM per device.

v0:
```python
import math
import jax
import jax.numpy as jnp
from jax import lax
from jax.sharding import PartitionSpec as P

DAMPING = 0.1


def extended(value, sides, width):
    for axis, dim in sides:
        size, length = (lax.axis_size(axis), value.shape[dim])
        up = [(i, (i + 1) % size) for i in range(size - 1)]
        down = [(j, i) for i, j in up]
        last = lax.slice_in_dim(value, length - width, length, axis=dim)
        initial = lax.slice_in_dim(value, 0, width, axis=dim)
        before = lax.ppermute(last, axis, up)
        after = lax.ppermute(initial, axis, down)
        value = jnp.concatenate([before, value, after], axis=dim)
    return value


def add_columns(segment, operand):
    return jnp.dot(operand, segment, preferred_element_type=jnp.float32)


def add_with_norms(segment, operand):
    summed = add_columns(segment, operand)
    squares = jnp.sum(jnp.square(segment.astype(jnp.float32)), axis=0)
    return (summed, squares)


def contract_rows(left_side, right_side):
    return lax.dot_general(
        left_side, right_side, (((0,), (0,)), ((), ())), preferred_element_type=jnp.float32
    )


def per_device(acts, conv_weight, conv_bias, out_cotangent, basis_in, basis_out, query_ids):
    ex_local, band_rows, band_cols, channels = acts.shape
    padded = extended(acts, (("space", 1),), 1)
    padded = jnp.pad(padded, ((0, 0), (0, 0), (1, 1), (0, 0)))
    shifted = [
        padded[:, row_shift : row_shift + band_rows, col_shift : col_shift + band_cols, :]
        for row_shift in range(3)
        for col_shift in range(3)
    ]
    positions = ex_local * band_rows * band_cols
    patches = jnp.stack(shifted, axis=3).reshape(positions, 9 * channels)
    kernel_cols = lax.all_gather(conv_weight, "batch", axis=0, tiled=True)
    preact = jnp.dot(
        patches,
        lax.all_gather(kernel_cols, "space", axis=1, tiled=True),
        preferred_element_type=jnp.float32,
    )
    preact = preact + conv_bias
    sigmoid_pre = jax.nn.sigmoid(preact)
    activated = (preact * sigmoid_pre).astype(jnp.bfloat16).reshape(acts.shape)
    grad_pre = (
        out_cotangent.reshape(positions, channels).astype(jnp.float32)
        * sigmoid_pre
        * (1.0 + preact * (1.0 - sigmoid_pre))
    ).astype(jnp.bfloat16)
    basis_rank = basis_in.shape[1]
    probe_in = add_columns(lax.all_gather(basis_in, "batch", axis=0, tiled=True), patches).astype(
        jnp.bfloat16
    )
    probe_out = add_columns(
        lax.all_gather(basis_out, "batch", axis=0, tiled=True), grad_pre
    ).astype(jnp.bfloat16)
    term_in = contract_rows(patches, probe_in)
    term_out = contract_rows(grad_pre, probe_out)
    summed = lax.psum((term_in, term_out), "space")
    owned_in, owned_out = (
        lax.psum_scatter(summed[0], "batch", scatter_dimension=0, tiled=True),
        lax.psum_scatter(summed[1], "batch", scatter_dimension=0, tiled=True),
    )
    total_positions = positions * lax.axis_size("batch") * lax.axis_size("space")
    basis_in_new = (owned_in / total_positions).astype(jnp.bfloat16)
    basis_out_new = (owned_out / total_positions).astype(jnp.bfloat16)
    raw_in, square_in = add_with_norms(
        lax.all_gather(basis_in_new, "batch", axis=0, tiled=True), patches
    )
    raw_out, square_out = add_with_norms(
        lax.all_gather(basis_out_new, "batch", axis=0, tiled=True), grad_pre
    )
    scale_in = jnp.sqrt(square_in)
    scale_out = jnp.sqrt(square_out)
    feat_in = (
        (raw_in / scale_in)
        .astype(jnp.bfloat16)
        .reshape(ex_local, band_rows * band_cols, basis_rank)
    )
    feat_out = (
        (raw_out / scale_out)
        .astype(jnp.bfloat16)
        .reshape(ex_local, band_rows * band_cols, basis_rank)
    )
    height = band_rows * lax.axis_size("space")
    projected = (
        jnp.einsum("epi,epj->eij", feat_out, feat_in, preferred_element_type=jnp.float32) / height
    )
    projected = lax.psum(projected, "space")
    scaled = projected / (scale_out[:, None] * scale_in[None, :] + DAMPING)
    all_projs = lax.all_gather(projected, "batch", axis=0, tiled=True)
    queries = jnp.take(all_projs, query_ids, axis=0)
    scores = jnp.einsum("qij,eij->qe", queries, scaled, precision=lax.Precision.HIGHEST) / (
        basis_rank * math.sqrt(basis_rank)
    )
    return (activated, basis_in_new, scores)


def solution(mesh):
    return jax.shard_map(
        per_device,
        mesh=mesh,
        in_specs=(
            P("batch", "space", None, None),
            P("batch", "space"),
            P(),
            P("batch", "space", None, None),
            P("batch", None),
            P("batch", None),
            P(),
        ),
        out_specs=(P("batch", "space", None, None), P("batch", None), P(None, "batch")),
        check_vma=False,
    )
```

profile of v0, /device:TPU:1, one launch (start us, length us, event | category | flops | bytes accessed | tf_op | source)
XLA Modules:
  0.0 1847.2 jit_solution(3337683036946885710)
XLA Ops:
  7.2 0.0 all-gather.8.cloned.1.call-start
  7.2 132.7 %all-gather = bf16[64,90,80]{1,2,0:T(8,128)(2,1)S(1)} all-gather(bf16[1,90,80]{1,2,0:T(8,128)(2,1)} %bitcast.90), channel_id=1, replica_groups=mesh['batch'=64,'space'=8] {'batch'}, dimensions={0}, use_global_device_ids=true | all-gather | bytes 936000 | tf_op jit(solution)/shard_map/all_gather | solution.py:50
  139.9 0.0 copy-start
  139.9 0.0 copy-start.4
  140.0 0.0 copy-start.5
  140.0 0.3 copy.15
  140.3 2.8 reshape.103
  143.1 0.0 all-gather.8.cloned.1.call-update
  143.1 0.0 all-reduce.7.cloned.1.call-start
  143.1 0.0 copy-done
  143.2 8.0 collective-permute-start
  151.2 1.3 collective-permute-start.1
  152.5 0.0 copy-done.4
  152.5 167.6 %all-gather.1 = bf16[64,90,64]{1,2,0:T(8,128)(2,1)S(1)} all-gather(bf16[1,90,64]{1,2,0:T(8,128)(2,1)S(1)} %bitcast.91), channel_id=1, replica_groups=mesh['batch'=64,'space'=8] {'batch'}, dimensions={0}, use_global_device_ids=true | all-gather | bytes 748800 | tf_op jit(solution)/shard_map/all_gather | solution.py:65
  320.1 0.0 copy-done.5
  320.1 165.3 %all-gather.2 = bf16[64,10,64]{2,1,0:T(8,128)(2,1)S(1)} all-gather(bf16[1,10,64]{2,1,0:T(8,128)(2,1)S(1)} %bitcast.92), channel_id=1, replica_groups=mesh['batch'=64,'space'=8] {'batch'}, dimensions={0}, use_global_device_ids=true | all-gather | bytes 83200 | tf_op jit(solution)/shard_map/all_gather | solution.py:69
  485.4 0.1 reshape.107
  485.5 0.7 copy.16
  486.2 2.4 reshape.105
  488.6 0.0 collective-permute-done
  488.6 0.0 copy-start.1
  488.6 0.0 collective-permute-done.1
  488.6 0.6 copy-done.1
  489.2 0.2 fusion.16
  489.4 0.9 fusion.25
  490.4 0.1 fusion.23
  490.6 0.1 fusion.21
  490.8 0.1 fusion.17
  490.9 2.0 copy.14
  492.9 0.9 copy.22
  493.7 0.0 copy-start.6
  493.7 4.5 fusion.3
  498.3 0.0 all-gather.8.cloned.1.call-done
  498.3 0.0 copy-done.6
  498.3 6.4 fusion.11
  504.7 1.3 fusion.2
  506.0 0.0 all-reduce.7.cloned.1.call-update
  506.0 0.0 all-gather.10.cloned.1.call-start
  506.1 1.3 dynamic-slice
  508.6 821.8 %all-reduce.7.cloned.1.call-done = (f32[5760,64]{0,1:T(8,128)}, f32[640,64]{1,0:T(8,128)}) async-done(((f32[5760,64]{0,1:T(8,128)}, f32[640,64]{1,0:T(8,128)}), (f32[5760,64]{0,1:T(8,128)}, f32[640,64]{1,0:T(8,128)})) %all-reduce.7.cloned.1.call-update) | async-done | bytes 1638416
  1330.4 0.9 constant_dynamic-slice_fusion.1
  1331.3 0.7 constant_dynamic-slice_fusion
  1332.0 66.9 %all-reduce.4 = (f32[90,64]{0,1:T(8,128)S(1)}, f32[10,64]{1,0:T(8,128)S(1)}) all-reduce(f32[90,64]{0,1:T(8,128)S(1)} %constant_dynamic-slice_fusion.1, f32[10,64]{1,0:T(8,128)S(1)} %constant_dynamic-slice_fusion), channel_id=1, replica_groups=mesh['batch'=64,'space'=8] {'space'}, use_global_device_ids=true, to_apply=%region_0.1 | all-reduce | flops 6400 | bytes 51200 | tf_op jit(solution)/shard_map/psum | solution.py:73
  1398.9 0.0 copy-start.2
  1398.9 130.7 %all-gather.4 = bf16[64,90,64]{1,2,0:T(8,128)(2,1)S(1)} all-gather(bf16[1,90,64]{1,2,0:T(8,128)(2,1)S(1)} %fusion.45), channel_id=1, replica_groups=mesh['batch'=64,'space'=8] {'batch'}, dimensions={0}, use_global_device_ids=true | all-gather | bytes 748800 | tf_op jit(solution)/shard_map/all_gather | solution.py:82
  1529.6 1.6 copy.17
  1531.2 3.1 reshape.111
  1534.4 1.4 multiply_reduce_fusion
  1535.7 0.0 copy-done.2
  1535.8 114.8 %all-gather.3 = bf16[64,10,64]{2,1,0:T(8,128)(2,1)S(1)} all-gather(bf16[1,10,64]{2,1,0:T(8,128)(2,1)S(1)} %fusion.29), channel_id=1, replica_groups=mesh['batch'=64,'space'=8] {'batch'}, dimensions={0}, use_global_device_ids=true | all-gather | bytes 83200 | tf_op jit(solution)/shard_map/all_gather | solution.py:85
  1650.5 0.7 reshape.109
  1651.3 1.0 multiply_reduce_fusion.1
  1652.3 1.2 fusion.1
  1653.5 2.3 fusion.6
  1655.7 60.8 %psum.23 = f32[1,64,64]{2,1,0:T(8,128)} all-reduce(f32[1,64,64]{2,1,0:T(8,128)S(1)} %fusion.6), channel_id=1, replica_groups=mesh['batch'=64,'space'=8] {'space'}, use_global_device_ids=true, to_apply=%region_6.7 | all-reduce | flops 4096 | bytes 32768 | tf_op jit(solution)/shard_map/psum | solution.py:103
  1716.5 0.0 all-gather.10.cloned.1.call-update
  1716.6 0.0 copy-done.7
  1716.6 0.0 copy-done.3
  1716.6 0.6 multiply_convert_fusion.1
  1717.2 0.8 add_divide_fusion.1
  1718.1 119.1 %all-gather.10.cloned.1.call-done = f32[64,64,64]{2,1,0:T(8,128)} async-done(((f32[1,64,64]{2,1,0:T(8,128)}), f32[64,64,64]{2,1,0:T(8,128)}) %all-gather.10.cloned.1.call-update) | async-done | bytes 1048592 | tf_op jit(solution)/shard_map/all_gather | solution.py:105
  1837.2 2.2 gather_fusion
  1839.4 0.1 broadcast_select_fusion
  1839.5 1.2 fusion.8
  (15 shorter events, 0.3 us)
Async XLA Ops:
  7.2 491.1 %all-gather.8.cloned.1.call-start = ((), (), s32[]{:S(2)}) async-start(), calls=%async_computation | async-start | bytes 8294400 | tf_op jit(solution)/shard_map/all_gather | solution.py:53
  139.9 3.2 copy-start
  139.9 12.6 copy-start.4
  140.0 180.1 %copy-start.5 = (bf16[10,64]{1,0:T(8,128)(2,1)S(1)}, bf16[10,64]{1,0:T(8,128)(2,1)}, u32[]{:S(2)}) copy-start(bf16[10,64]{1,0:T(8,128)(2,1)} %param.12) | copy-start | bytes 3844
  143.1 1187.3 %all-reduce.7.cloned.1.call-start = ((), (), s32[]{:S(2)}) async-start(), calls=%async_computation.2 | async-start | bytes 3604480
  143.2 345.4 %collective-permute-start = (bf16[1,1,64,640]{3,2,1,0:T(8,128)(2,1)S(1)}, bf16[1,1,64,640]{3,2,1,0:T(8,128)(2,1)S(1)}, u32[]{:S(2)}, u32[]{:S(2)}) collective-permute-start(bf16[1,1,64,640]{3,2,1,0:T(8,128)(2,1)S(1)} %get-tuple-element.9), channel_id=1, source_target_pairs={{0,1},{1,2},{2,3},{3,4},{4,5},{5,6},{6,7},{8,9},{9,10},{10,11},{11... | collective-permute-start | bytes 245768 | tf_op jit(solution)/shard_map/ppermute | solution.py:17
  151.2 337.4 %collective-permute-start.1 = (bf16[1,1,64,640]{3,2,1,0:T(8,128)(2,1)S(1)}, bf16[1,1,64,640]{3,2,1,0:T(8,128)(2,1)S(1)}, u32[]{:S(2)}, u32[]{:S(2)}) collective-permute-start(bf16[1,1,64,640]{3,2,1,0:T(8,128)(2,1)S(1)} %get-tuple-element.10), channel_id=1, source_target_pairs={{1,0},{2,1},{3,2},{4,3},{5,4},{6,5},{7,6},{9,8},{10,9},{11,10},{12... | collective-permute-start | bytes 245768 | tf_op jit(solution)/shard_map/ppermute | solution.py:18
  488.6 0.6 copy-start.1
  493.7 4.6 copy-start.6
  506.0 1331.2 %all-gather.10.cloned.1.call-start = ((), (), s32[]{:S(2)}) async-start(), calls=%async_computation.1 | async-start | bytes 2129920 | tf_op jit(solution)/shard_map/all_gather | solution.py:105
  1398.9 136.8 %copy-start.2 = (f32[90,64]{0,1:T(8,128)}, f32[90,64]{0,1:T(8,128)S(1)}, u32[]{:S(2)}) copy-start(f32[90,64]{0,1:T(8,128)S(1)} %get-tuple-element.5) | copy-start | bytes 69124
  1534.4 182.2 %copy-start.7 = (s32[8]{0:T(128)S(1)}, s32[8]{0:T(128)}, u32[]{:S(2)}) copy-start(s32[8]{0:T(128)} %param.13) | copy-start | bytes 100
  1651.3 65.3 %copy-start.3 = (f32[90,64]{0,1:T(8,128)S(1)}, f32[90,64]{0,1:T(8,128)}, u32[]{:S(2)}) copy-start(f32[90,64]{0,1:T(8,128)} %copy-done.2) | copy-start | bytes 69124
Sparse Core Ops, SparseCore 0:
  143.2 265.6 all-gather.7
  506.1 824.2 all-reduce.6
  1716.7 120.4 all-gather.9
where the time goes:
time: 1850 us
  waiting for transfers between devices  941 us (51%)
  blocking collectives  839 us (45%)
  local copies, waits for them, and re-layouts  20.8 us (1%)
    unnamed x4, waiting for transfers between devices  822 us
    all_gather x1, blocking collectives, per_device(): lax.all_gather(basis_in, 'batch', axis=0, tiled=True)  168 us
    all_gather x1, blocking collectives, per_device(): lax.all_gather(basis_out, 'batch', axis=0, tiled=True)  165 us
    all_gather x1, blocking collectives, per_device(): kernel_cols = lax.all_gather(conv_weight, 'batch', axis=0, tiled=True)  133 us
    all_gather x1, blocking collectives, per_device(): lax.all_gather(basis_in_new, 'batch', axis=0, tiled=True)  131 us
    all_gather x1, waiting for transfers between devices, per_device(): all_projs = lax.all_gather(projected, 'batch', axis=0, tiled=True)  119 us
    all_gather x1, blocking collectives, per_device(): lax.all_gather(basis_out_new, 'batch', axis=0, tiled=True)  115 us
    psum x1, blocking collectives, per_device(): summed = lax.psum((term_in, term_out), 'space')  66.9 us
  transfers between devices with their start and end apart: 5, of which 2 were waited for; matrix products, arithmetic and copies ran while one was open for 1% of the time, Pallas kernels for 0%

commit v1 on v0

--- a/solution.py
+++ b/solution.py
@@ -100,7 +100,8 @@
     projected = (
         jnp.einsum("epi,epj->eij", feat_out, feat_in, preferred_element_type=jnp.float32) / height
     )
-    projected = lax.psum(projected, "space")
+    parts = lax.all_gather(projected, "space", axis=0, tiled=False)
+    projected = parts.sum(axis=0)
     scaled = projected / (scale_out[:, None] * scale_in[None, :] + DAMPING)
     all_projs = lax.all_gather(projected, "batch", axis=0, tiled=True)
     queries = jnp.take(all_projs, query_ids, axis=0)

time: 1850 us -> 1840 us (level)
    psum x1 -> x0, blocking collectives: 60.8 us -> none  [per_device(): projected = lax.psum(projected, 'space')]
    all_gather x0 -> x1, blocking collectives: none -> 57.2 us  [per_device(): parts = lax.all_gather(projected, 'space', axis=0, tiled=False)]
where the time goes in v1:
time: 1840 us
  waiting for transfers between devices  936 us (51%)
  blocking collectives  836 us (45%)
  local copies, waits for them, and re-layouts  20.8 us (1%)
    unnamed x4, waiting for transfers between devices  822 us
    all_gather x1, blocking collectives, per_device(): lax.all_gather(basis_in, 'batch', axis=0, tiled=True)  168 us
    all_gather x1, blocking collectives, per_device(): lax.all_gather(basis_out, 'batch', axis=0, tiled=True)  165 us
    all_gather x1, blocking collectives, per_device(): kernel_cols = lax.all_gather(conv_weight, 'batch', axis=0, tiled=True)  133 us
    all_gather x1, blocking collectives, per_device(): lax.all_gather(basis_in_new, 'batch', axis=0, tiled=True)  131 us
    all_gather x1, blocking collectives, per_device(): lax.all_gather(basis_out_new, 'batch', axis=0, tiled=True)  115 us
    all_gather x1, waiting for transfers between devices, per_device(): all_projs = lax.all_gather(projected, 'batch', axis=0, tiled=True)  114 us
    psum x1, blocking collectives, per_device(): summed = lax.psum((term_in, term_out), 'space')  66.9 us
  transfers between devices with their start and end apart: 5, of which 2 were waited for; matrix products, arithmetic and copies ran while one was open for 1% of the time, Pallas kernels for 0%

profile of v1, /device:TPU:1, one launch (start us, length us, event | category | flops | bytes accessed | tf_op | source)
XLA Modules:
  0.0 1839.6 jit_solution(14985259563659888838)
XLA Ops:
  7.2 0.0 all-gather.10.cloned.1.call-start
  7.2 132.7 %all-gather.2 = bf16[64,90,80]{1,2,0:T(8,128)(2,1)S(1)} all-gather(bf16[1,90,80]{1,2,0:T(8,128)(2,1)} %bitcast.91), channel_id=1, replica_groups=mesh['batch'=64,'space'=8] {'batch'}, dimensions={0}, use_global_device_ids=true | all-gather | bytes 936000 | tf_op jit(solution)/shard_map/all_gather | solution.py:50
  139.9 0.0 copy-start
  139.9 0.0 copy-start.4
  140.0 0.0 copy-start.5
  140.0 0.3 copy.15
  140.3 2.8 reshape.79
  143.1 0.0 all-gather.10.cloned.1.call-update
  143.1 0.0 all-reduce.7.cloned.1.call-start
  143.1 0.0 copy-done
  143.2 8.0 collective-permute-start
  151.2 1.3 collective-permute-start.1
  152.5 0.0 copy-done.4
  152.5 167.6 %all-gather.3 = bf16[64,90,64]{1,2,0:T(8,128)(2,1)S(1)} all-gather(bf16[1,90,64]{1,2,0:T(8,128)(2,1)S(1)} %bitcast.92), channel_id=1, replica_groups=mesh['batch'=64,'space'=8] {'batch'}, dimensions={0}, use_global_device_ids=true | all-gather | bytes 748800 | tf_op jit(solution)/shard_map/all_gather | solution.py:65
  320.1 0.0 copy-done.5
  320.1 165.3 %all-gather.4 = bf16[64,10,64]{2,1,0:T(8,128)(2,1)S(1)} all-gather(bf16[1,10,64]{2,1,0:T(8,128)(2,1)S(1)} %bitcast.93), channel_id=1, replica_groups=mesh['batch'=64,'space'=8] {'batch'}, dimensions={0}, use_global_device_ids=true | all-gather | bytes 83200 | tf_op jit(solution)/shard_map/all_gather | solution.py:69
  485.4 0.1 reshape.83
  485.5 0.7 copy.16
  486.2 2.4 reshape.81
  488.6 0.0 collective-permute-done
  488.6 0.0 copy-start.1
  488.6 0.0 collective-permute-done.1
  488.6 0.6 copy-done.1
  489.2 0.2 fusion.15
  489.4 0.9 fusion.24
  490.4 0.1 fusion.22
  490.6 0.1 fusion.20
  490.8 0.1 fusion.16
  490.9 2.0 copy.14
  492.9 0.9 copy.22
  493.7 0.0 copy-start.6
  493.7 4.5 fusion.3
  498.3 0.0 copy-done.6
  498.3 6.4 fusion.10
  504.7 1.3 fusion.2
  506.0 0.0 all-reduce.7.cloned.1.call-update
  506.0 0.0 all-gather.12.cloned.1.call-start
  506.1 1.3 dynamic-slice
  508.6 821.8 %all-reduce.7.cloned.1.call-done = (f32[5760,64]{0,1:T(8,128)}, f32[640,64]{1,0:T(8,128)}) async-done(((f32[5760,64]{0,1:T(8,128)}, f32[640,64]{1,0:T(8,128)}), (f32[5760,64]{0,1:T(8,128)}, f32[640,64]{1,0:T(8,128)})) %all-reduce.7.cloned.1.call-update) | async-done | bytes 1638416
  1330.4 0.9 constant_dynamic-slice_fusion.1
  1331.3 0.7 constant_dynamic-slice_fusion
  1332.0 66.9 %all-reduce.4 = (f32[90,64]{0,1:T(8,128)S(1)}, f32[10,64]{1,0:T(8,128)S(1)}) all-reduce(f32[90,64]{0,1:T(8,128)S(1)} %constant_dynamic-slice_fusion.1, f32[10,64]{1,0:T(8,128)S(1)} %constant_dynamic-slice_fusion), channel_id=1, replica_groups=mesh['batch'=64,'space'=8] {'space'}, use_global_device_ids=true, to_apply=%region_0.1 | all-reduce | flops 6400 | bytes 51200 | tf_op jit(solution)/shard_map/psum | solution.py:73
  1398.9 130.7 %all-gather.6 = bf16[64,90,64]{1,2,0:T(8,128)(2,1)S(1)} all-gather(bf16[1,90,64]{1,2,0:T(8,128)(2,1)S(1)} %fusion.44), channel_id=1, replica_groups=mesh['batch'=64,'space'=8] {'batch'}, dimensions={0}, use_global_device_ids=true | all-gather | bytes 748800 | tf_op jit(solution)/shard_map/all_gather | solution.py:82
  1529.6 1.6 copy.17
  1531.2 3.1 reshape.87
  1534.4 1.4 multiply_reduce_fusion
  1535.7 0.0 copy-start.7
  1535.7 0.0 copy-done.2
  1535.8 115.3 %all-gather.5 = bf16[64,10,64]{2,1,0:T(8,128)(2,1)S(1)} all-gather(bf16[1,10,64]{2,1,0:T(8,128)(2,1)S(1)} %fusion.28), channel_id=1, replica_groups=mesh['batch'=64,'space'=8] {'batch'}, dimensions={0}, use_global_device_ids=true | all-gather | bytes 83200 | tf_op jit(solution)/shard_map/all_gather | solution.py:85
  1651.0 0.7 reshape.85
  1651.8 1.0 multiply_reduce_fusion.1
  1652.8 1.2 fusion.1
  1654.0 2.3 fusion.5
  1656.2 57.2 %all-gather = f32[512,64]{1,0:T(8,128)S(1)} all-gather(f32[64,64]{1,0:T(8,128)S(1)} %fusion.5), channel_id=2, replica_groups=mesh['batch'=64,'space'=8] {'space'}, dimensions={0}, use_global_device_ids=true | all-gather | bytes 147456 | tf_op jit(solution)/shard_map/all_gather | solution.py:103
  1713.5 0.6 reduce.1
  1714.1 0.0 all-gather.12.cloned.1.call-update
  1714.1 0.0 copy-done.7
  1714.2 0.0 copy-done.3
  1714.2 0.6 multiply_convert_fusion.1
  1714.8 0.8 add_divide_fusion.1
  1715.7 113.9 %all-gather.12.cloned.1.call-done = f32[4096,64]{1,0:T(8,128)} async-done(((f32[64,64]{1,0:T(8,128)}), f32[4096,64]{1,0:T(8,128)}) %all-gather.12.cloned.1.call-update) | async-done | bytes 1048592 | tf_op jit(solution)/shard_map/all_gather | solution.py:106
  1829.6 2.2 gather_fusion
  1831.7 0.1 broadcast_select_fusion
  1831.8 1.2 fusion.7
  (16 shorter events, 0.3 us)
Async XLA Ops:
  7.2 491.1 %all-gather.10.cloned.1.call-start = ((), (), s32[]{:S(2)}) async-start(), calls=%async_computation | async-start | bytes 8294400 | tf_op jit(solution)/shard_map/all_gather | solution.py:53
  139.9 3.2 copy-start
  139.9 12.6 copy-start.4
  140.0 180.1 %copy-start.5 = (bf16[10,64]{1,0:T(8,128)(2,1)S(1)}, bf16[10,64]{1,0:T(8,128)(2,1)}, u32[]{:S(2)}) copy-start(bf16[10,64]{1,0:T(8,128)(2,1)} %param.12) | copy-start | bytes 3844
  143.1 1187.3 %all-reduce.7.cloned.1.call-start = ((), (), s32[]{:S(2)}) async-start(), calls=%async_computation.2 | async-start | bytes 3604480
  143.2 345.4 %collective-permute-start = (bf16[1,1,64,640]{3,2,1,0:T(8,128)(2,1)S(1)}, bf16[1,1,64,640]{3,2,1,0:T(8,128)(2,1)S(1)}, u32[]{:S(2)}, u32[]{:S(2)}) collective-permute-start(bf16[1,1,64,640]{3,2,1,0:T(8,128)(2,1)S(1)} %get-tuple-element.9), channel_id=1, source_target_pairs={{0,1},{1,2},{2,3},{3,4},{4,5},{5,6},{6,7},{8,9},{9,10},{10,11},{11... | collective-permute-start | bytes 245768 | tf_op jit(solution)/shard_map/ppermute | solution.py:17
  151.2 337.4 %collective-permute-start.1 = (bf16[1,1,64,640]{3,2,1,0:T(8,128)(2,1)S(1)}, bf16[1,1,64,640]{3,2,1,0:T(8,128)(2,1)S(1)}, u32[]{:S(2)}, u32[]{:S(2)}) collective-permute-start(bf16[1,1,64,640]{3,2,1,0:T(8,128)(2,1)S(1)} %get-tuple-element.10), channel_id=1, source_target_pairs={{1,0},{2,1},{3,2},{4,3},{5,4},{6,5},{7,6},{9,8},{10,9},{11,10},{12... | collective-permute-start | bytes 245768 | tf_op jit(solution)/shard_map/ppermute | solution.py:18
  488.6 0.6 copy-start.1
  493.7 4.6 copy-start.6
  506.0 1323.5 %all-gather.12.cloned.1.call-start = ((), (), s32[]{:S(2)}) async-start(), calls=%async_computation.1 | async-start | bytes 2129920 | tf_op jit(solution)/shard_map/all_gather | solution.py:106
  1398.9 136.8 %copy-start.2 = (f32[90,64]{0,1:T(8,128)}, f32[90,64]{0,1:T(8,128)S(1)}, u32[]{:S(2)}) copy-start(f32[90,64]{0,1:T(8,128)S(1)} %get-tuple-element.5) | copy-start | bytes 69124
  1535.7 178.4 %copy-start.7 = (s32[8]{0:T(128)S(1)}, s32[8]{0:T(128)}, u32[]{:S(2)}) copy-start(s32[8]{0:T(128)} %param.13) | copy-start | bytes 100
  1651.8 62.4 %copy-start.3 = (f32[90,64]{0,1:T(8,128)S(1)}, f32[90,64]{0,1:T(8,128)}, u32[]{:S(2)}) copy-start(f32[90,64]{0,1:T(8,128)} %copy-done.2) | copy-start | bytes 69124
Sparse Core Ops, SparseCore 0:
  143.2 265.6 all-gather.9
  506.1 824.2 all-reduce.6
  1714.3 115.2 all-gather.11
